TPU v7x, 512 devices: a whole 4x8x8 slice. The times are simulated.
512 devices in a mesh: wide: 64 (over y, z), narrow: 8 (over x, core).
Axes of the slice: x: 4, y: 8, z: 8, core: 2. Of those that a mesh axis runs over, the one named last changes fastest.
Arguments:
- right_side: bfloat16 [4, 1024, 512], P(None, 'wide'), may hold values from -6 to 6
- partial_in: float32 [8, 4, 1024, 512], P('narrow', None, 'wide'), may hold values from -6 to 6
- window_factor: bfloat16 [4, 1024, 4, 1024], P(None, 'wide', None, 'narrow'), may hold values from -0.09375 to 0.09375
- inverse_t: bfloat16 [4, 1024, 1024], P(None, 'wide', 'narrow'), as said below
- trailing_factor: bfloat16 [131072, 4, 1024], P('wide', None, 'narrow'), may hold values from -0.09375 to 0.09375
Outputs:
- solved: bfloat16 [4, 1024, 512], P(None, 'narrow')
- trailing: float32 [131072, 512], P(('wide', 'narrow'))
Inputs may be any that keep to these rules, and one draw needn't show every extreme that they name: inverse_t[k] is the transpose of the inverse of the k-th diagonal block of the lower-triangular factor: entry [k, j, i] is zero where j > i.
All inputs are finite; a program needn't handle non-finite values.
Results may differ from a plain program's by a relative error of at most 0.012.
Values may be sent and summed in bfloat16 or wider, within the bound.
No kernel may reach another device: no remote copies, remote signals or barrier semaphores. Data moves between devices by JAX's collectives and lax.ppermute only.
A program may use at most 64 MiB of HBM per device.

v0:
```python
import jax
import jax.numpy as jnp
from jax import lax
from jax.sharding import PartitionSpec as P


def per_device(right_side, partial_in, window_factor, inverse_t, trailing_factor):
    steps_count = right_side.shape[0]
    col_width = inverse_t.shape[2]
    rhs_width = right_side.shape[2]
    trail_rows = trailing_factor.shape[0]
    solved_list = []
    for block in range(steps_count):
        fanned = partial_in[0, block]
        for prior in range(block):
            fanned = fanned + jnp.dot(
                window_factor[block, :, prior, :],
                solved_list[prior],
                preferred_element_type=jnp.float32,
            )
        fanned = lax.psum(fanned, "narrow")
        residue = (right_side[block].astype(jnp.float32) - fanned).astype(jnp.bfloat16)
        solution = lax.dot_general(
            lax.all_gather(inverse_t[block], "wide", axis=0, tiled=True),
            lax.all_gather(residue, "wide", axis=0, tiled=True),
            (((0,), (0,)), ((), ())),
            preferred_element_type=jnp.float32,
        )
        solution = solution.astype(jnp.bfloat16)
        solved_list.append(solution)
    solved = jnp.stack(solved_list)
    flat_factor = trailing_factor.reshape(trail_rows, steps_count * col_width)
    flat_solved = solved.reshape(steps_count * col_width, rhs_width)
    trailing = lax.psum_scatter(
        jnp.dot(flat_factor, flat_solved, preferred_element_type=jnp.float32),
        "narrow",
        scatter_dimension=0,
        tiled=True,
    )
    return (solved, trailing)


def solution(mesh):
    placed = (
        P(None, "wide", None),
        P("narrow", None, "wide", None),
        P(None, "wide", None, "narrow"),
        P(None, "wide", "narrow"),
        P("wide", None, "narrow"),
    )
    return jax.shard_map(
        per_device,
        mesh=mesh,
        in_specs=placed,
        out_specs=(P(None, "narrow", None), P(("wide", "narrow"), None)),
        check_vma=False,
    )
```

profile of v0, /device:TPU:8, one launch (start us, length us, event | category | flops | bytes accessed | tf_op | source)
XLA Modules:
  0.0 483.0 jit_solution(5871402175136502424)
XLA Ops:
  7.2 0.9 slice_bitcast_fusion
  8.2 25.6 %psum.28 = f32[16,512]{1,0:T(8,128)S(1)} all-reduce(f32[16,512]{1,0:T(8,128)S(1)} %slice_bitcast_fusion), channel_id=1, replica_groups=mesh['wide'=64,'narrow'=8] {'narrow'}, use_global_device_ids=true, to_apply=%region_0.0 | all-reduce | flops 8192 | bytes 65536 | tf_op jit(solution)/shard_map/psum | solution.py:21
  33.8 1.3 fusion.15
  35.9 56.0 %all-gather = bf16[1,1024,128]{2,1,0:T(8,128)(2,1)S(1)} all-gather(bf16[1,16,128]{2,1,0:T(8,128)(2,1)S(1)} %get-tuple-element.14), channel_id=2, replica_groups=mesh['wide'=64,'narrow'=8] {'wide'}, dimensions={1}, use_global_device_ids=true | all-gather | bytes 266240 | tf_op jit(solution)/shard_map/all_gather | solution.py:24
  91.9 0.9 fusion.16
  92.8 26.1 %all-gather.9.cloned.1.call-done = bf16[1024,512]{1,0:T(8,128)(2,1)} async-done(((bf16[16,512]{1,0:T(8,128)(2,1)}), bf16[1024,512]{1,0:T(8,128)(2,1)}) %all-gather.9.cloned.1.call-update) | async-done | bytes 1048592 | tf_op jit(solution)/shard_map/all_gather | solution.py:25
  118.9 1.7 convolution_convert_fusion.3
  120.6 0.9 fusion.7
  121.5 23.6 %psum.29 = f32[16,512]{1,0:T(8,128)S(1)} all-reduce(f32[16,512]{1,0:T(8,128)S(1)} %fusion.7), channel_id=1, replica_groups=mesh['wide'=64,'narrow'=8] {'narrow'}, use_global_device_ids=true, to_apply=%region_1.0 | all-reduce | flops 8192 | bytes 65536 | tf_op jit(solution)/shard_map/psum | solution.py:21
  145.8 48.2 %all-gather.1 = bf16[1,1024,128]{2,1,0:T(8,128)(2,1)S(1)} all-gather(bf16[1,16,128]{2,1,0:T(8,128)(2,1)S(1)} %get-tuple-element.13), channel_id=3, replica_groups=mesh['wide'=64,'narrow'=8] {'wide'}, dimensions={1}, use_global_device_ids=true | all-gather | bytes 266240 | tf_op jit(solution)/shard_map/all_gather | solution.py:24
  194.2 28.4 %all-gather.11.cloned.1.call-done = bf16[1024,512]{1,0:T(8,128)(2,1)} async-done(((bf16[16,512]{1,0:T(8,128)(2,1)}), bf16[1024,512]{1,0:T(8,128)(2,1)}) %all-gather.11.cloned.1.call-update) | async-done | bytes 1048592 | tf_op jit(solution)/shard_map/all_gather | solution.py:25
  222.6 1.7 convolution_convert_fusion.2
  224.4 23.6 %psum.30 = f32[16,512]{1,0:T(8,128)S(1)} all-reduce(f32[16,512]{1,0:T(8,128)S(1)} %fusion.5), channel_id=1, replica_groups=mesh['wide'=64,'narrow'=8] {'narrow'}, use_global_device_ids=true, to_apply=%region_2.0 | all-reduce | flops 8192 | bytes 65536 | tf_op jit(solution)/shard_map/psum | solution.py:21
  248.7 48.2 %all-gather.2 = bf16[1,1024,128]{2,1,0:T(8,128)(2,1)S(1)} all-gather(bf16[1,16,128]{2,1,0:T(8,128)(2,1)S(1)} %get-tuple-element.15), channel_id=4, replica_groups=mesh['wide'=64,'narrow'=8] {'wide'}, dimensions={1}, use_global_device_ids=true | all-gather | bytes 266240 | tf_op jit(solution)/shard_map/all_gather | solution.py:24
  297.2 28.3 %all-gather.13.cloned.1.call-done = bf16[1024,512]{1,0:T(8,128)(2,1)} async-done(((bf16[16,512]{1,0:T(8,128)(2,1)}), bf16[1024,512]{1,0:T(8,128)(2,1)}) %all-gather.13.cloned.1.call-update) | async-done | bytes 1048592 | tf_op jit(solution)/shard_map/all_gather | solution.py:25
  325.5 1.7 convolution_convert_fusion.1
  327.4 23.6 %psum.31 = f32[16,512]{1,0:T(8,128)S(1)} all-reduce(f32[16,512]{1,0:T(8,128)S(1)} %fusion.2), channel_id=1, replica_groups=mesh['wide'=64,'narrow'=8] {'narrow'}, use_global_device_ids=true, to_apply=%region_3.0 | all-reduce | flops 8192 | bytes 65536 | tf_op jit(solution)/shard_map/psum | solution.py:21
  351.7 48.2 %all-gather.3 = bf16[1,1024,128]{2,1,0:T(8,128)(2,1)S(1)} all-gather(bf16[1,16,128]{2,1,0:T(8,128)(2,1)S(1)} %get-tuple-element.12), channel_id=5, replica_groups=mesh['wide'=64,'narrow'=8] {'wide'}, dimensions={1}, use_global_device_ids=true | all-gather | bytes 266240 | tf_op jit(solution)/shard_map/all_gather | solution.py:24
  399.9 28.6 %all-gather.15.cloned.1.call-done = bf16[1024,512]{1,0:T(8,128)(2,1)} async-done(((bf16[16,512]{1,0:T(8,128)(2,1)}), bf16[1024,512]{1,0:T(8,128)(2,1)}) %all-gather.15.cloned.1.call-update) | async-done | bytes 1048592 | tf_op jit(solution)/shard_map/all_gather | solution.py:25
  428.5 1.7 fusion.1
  430.2 3.2 convolution_bitcast_fusion
  433.5 1.0 copy.17
  434.5 39.9 %reduce-scatter.2.cloned.1.call-done = f32[256,512]{0,1:T(8,128)} async-done(((f32[2048,512]{0,1:T(8,128)}), f32[256,512]{0,1:T(8,128)}) %reduce-scatter.2.cloned.1.call-update) | async-done | bytes 524304 | tf_op jit(solution)/shard_map/reduce_scatter | solution.py:34
  474.5 2.0 copy.18
  (26 shorter events, 3.7 us)
Async XLA Ops:
  7.2 423.0 %copy-start = (bf16[2048,4,128]{2,1,0:T(4,128)(2,1)S(1)}, bf16[2048,4,128]{2,1,0:T(4,128)(2,1)}, u32[]{:S(2)}) copy-start(bf16[2048,4,128]{2,1,0:T(4,128)(2,1)} %param.9) | copy-start | bytes 6291460
  7.2 186.8 %copy-start.1 = (f32[1,4,16,512]{3,2,1,0:T(8,128)S(1)}, f32[1,4,16,512]{3,2,1,0:T(8,128)}, u32[]{:S(2)}) copy-start(f32[1,4,16,512]{3,2,1,0:T(8,128)} %param.6) | copy-start | bytes 393220
  7.2 137.9 %copy-start.2 = (bf16[4,16,512]{2,1,0:T(8,128)(2,1)S(1)}, bf16[4,16,512]{2,1,0:T(8,128)(2,1)}, u32[]{:S(2)}) copy-start(bf16[4,16,512]{2,1,0:T(8,128)(2,1)} %param.5) | copy-start | bytes 196612
  7.2 111.7 %all-gather.9.cloned.1.call-start = ((), (), s32[]{:S(2)}) async-start(), calls=%async_computation.1 | async-start | bytes 1064960 | tf_op jit(solution)/shard_map/all_gather | solution.py:25
  35.1 187.4 %all-gather.11.cloned.1.call-start = ((), (), s32[]{:S(2)}) async-start(), calls=%async_computation.2 | async-start | bytes 1064960 | tf_op jit(solution)/shard_map/all_gather | solution.py:25
  145.7 179.8 %all-gather.13.cloned.1.call-start = ((), (), s32[]{:S(2)}) async-start(), calls=%async_computation.3 | async-start | bytes 1064960 | tf_op jit(solution)/shard_map/all_gather | solution.py:25
  248.7 179.8 %all-gather.15.cloned.1.call-start = ((), (), s32[]{:S(2)}) async-start(), calls=%async_computation.4 | async-start | bytes 1064960 | tf_op jit(solution)/shard_map/all_gather | solution.py:25
  351.6 122.8 %reduce-scatter.2.cloned.1.call-start = ((), (), s32[]{:S(2)}) async-start(), calls=%async_computation.5 | async-start | bytes 4718592 | tf_op jit(solution)/shard_map/reduce_scatter | solution.py:34
Sparse Core Ops, SparseCore 0:
  35.2 83.6 all-gather.8
  145.9 76.6 all-gather.10
  248.8 76.6 all-gather.12
  351.7 76.6 all-gather.14
  433.6 40.8 reduce-scatter.1
where the time goes:
time: 484 us; the launch traced here: 483 us
  blocking collectives  297 us (61%)
  waiting for transfers between devices  151 us (31%)
  between operations  13.9 us (3%)
  matrix products  11.7 us (2%)
  local copies, waits for them, and re-layouts  5.6 us (1%)
    all_gather x4, blocking collectives, per_device(): lax.all_gather(inverse_t[block], 'wide', axis=0, tiled=True)  201 us
    all_gather x4, waiting for transfers between devices, per_device(): lax.all_gather(residue, 'wide', axis=0, tiled=True)  111 us
    psum x4, blocking collectives, per_device(): fanned = lax.psum(fanned, 'narrow')  96.4 us
    reduce_scatter x1, waiting for transfers between devices, per_device(): lax.psum_scatter(jnp.dot(flat_factor, flat_solved, preferred_element_type...  39.9 us
  transfers between devices with their start and end apart: 5, of which 5 were waited for; matrix products, arithmetic and copies ran while one was open for 1% of the time, Pallas kernels for 0%

commit v1 on v0

--- a/solution.py
+++ b/solution.py
@@ -18,7 +18,8 @@
                 solved_list[prior],
                 preferred_element_type=jnp.float32,
             )
-        fanned = lax.psum(fanned, "narrow")
+        change_ports_for = lambda payload: jnp.sum(lax.all_gather(payload, "narrow"), axis=0)
+        fanned = change_ports_for(fanned)
         residue = (right_side[block].astype(jnp.float32) - fanned).astype(jnp.bfloat16)
         solution = lax.dot_general(
             lax.all_gather(inverse_t[block], "wide", axis=0, tiled=True),

time: 484 us -> 446 us (0.921)
  blocking collectives: 297 us -> 253 us
  waiting for transfers between devices: 151 us -> 158 us
    psum x4 -> x0, blocking collectives: 96.4 us -> none  [per_device(): fanned = lax.psum(fanned, 'narrow')]
    all_gather x0 -> x4, blocking collectives: none -> 52.6 us  [per_device(): lax.all_gather(payload, 'narrow')]
    all_gather x4, waiting for transfers between devices: 111 us -> 118 us  [per_device(): lax.all_gather(residue, 'wide', axis=0, tiled=True)]
where the time goes in v1:
time: 446 us
  blocking collectives  253 us (57%)
  waiting for transfers between devices  158 us (35%)
  between operations  13.9 us (3%)
  matrix products  10.9 us (2%)
  local copies, waits for them, and re-layouts  5.59 us (1%)
    all_gather x4, blocking collectives, per_device(): lax.all_gather(inverse_t[block], 'wide', axis=0, tiled=True)  201 us
    all_gather x4, waiting for transfers between devices, per_device(): lax.all_gather(residue, 'wide', axis=0, tiled=True)  118 us
    all_gather x4, blocking collectives, per_device(): lax.all_gather(payload, 'narrow')  52.6 us
    reduce_scatter x1, waiting for transfers between devices, per_device(): lax.psum_scatter(jnp.dot(flat_factor, flat_solved, preferred_element_type...  39.8 us
  transfers between devices with their start and end apart: 5, of which 5 were waited for; matrix products, arithmetic and copies ran while one was open for 1% of the time, Pallas kernels for 0%

profile of v1, /device:TPU:8, one launch (start us, length us, event | category | flops | bytes accessed | tf_op | source)
XLA Modules:
  0.0 445.7 jit_solution(13131205314668911513)
XLA Ops:
  7.2 0.9 slice.55
  8.2 13.2 %all-gather = f32[8,1,16,512]{3,2,1,0:T(8,128)S(1)} all-gather(f32[1,1,16,512]{3,2,1,0:T(8,128)S(1)} %slice.55), channel_id=2, replica_groups=mesh['wide'=64,'narrow'=8] {'narrow'}, dimensions={0}, use_global_device_ids=true | all-gather | bytes 294912 | tf_op jit(solution)/shard_map/all_gather | solution.py:21
  21.3 1.3 fusion.15
  22.8 0.7 fusion.17
  23.5 56.0 %all-gather.1 = bf16[1,1024,128]{2,1,0:T(8,128)(2,1)S(1)} all-gather(bf16[1,16,128]{2,1,0:T(8,128)(2,1)S(1)} %get-tuple-element.16), channel_id=3, replica_groups=mesh['wide'=64,'narrow'=8] {'wide'}, dimensions={1}, use_global_device_ids=true | all-gather | bytes 266240 | tf_op jit(solution)/shard_map/all_gather | solution.py:25
  79.5 0.9 fusion.16
  80.4 28.0 %all-gather.13.cloned.1.call-done = bf16[1024,512]{1,0:T(8,128)(2,1)} async-done(((bf16[16,512]{1,0:T(8,128)(2,1)}), bf16[1024,512]{1,0:T(8,128)(2,1)}) %all-gather.13.cloned.1.call-update) | async-done | bytes 1048592 | tf_op jit(solution)/shard_map/all_gather | solution.py:26
  108.3 1.7 convolution_convert_fusion.3
  110.2 13.1 %all-gather.2 = f32[128,512]{1,0:T(8,128)S(1)} all-gather(f32[16,512]{1,0:T(8,128)S(1)} %fusion.7), channel_id=4, replica_groups=mesh['wide'=64,'narrow'=8] {'narrow'}, dimensions={0}, use_global_device_ids=true | all-gather | bytes 294912 | tf_op jit(solution)/shard_map/all_gather | solution.py:21
  124.0 48.3 %all-gather.3 = bf16[1,1024,128]{2,1,0:T(8,128)(2,1)S(1)} all-gather(bf16[1,16,128]{2,1,0:T(8,128)(2,1)S(1)} %get-tuple-element.15), channel_id=5, replica_groups=mesh['wide'=64,'narrow'=8] {'wide'}, dimensions={1}, use_global_device_ids=true | all-gather | bytes 266240 | tf_op jit(solution)/shard_map/all_gather | solution.py:25
  172.5 30.2 %all-gather.15.cloned.1.call-done = bf16[1024,512]{1,0:T(8,128)(2,1)} async-done(((bf16[16,512]{1,0:T(8,128)(2,1)}), bf16[1024,512]{1,0:T(8,128)(2,1)}) %all-gather.15.cloned.1.call-update) | async-done | bytes 1048592 | tf_op jit(solution)/shard_map/all_gather | solution.py:26
  202.6 1.7 convolution_convert_fusion.2
  204.5 13.1 %all-gather.4 = f32[128,512]{1,0:T(8,128)S(1)} all-gather(f32[16,512]{1,0:T(8,128)S(1)} %fusion.5), channel_id=6, replica_groups=mesh['wide'=64,'narrow'=8] {'narrow'}, dimensions={0}, use_global_device_ids=true | all-gather | bytes 294912 | tf_op jit(solution)/shard_map/all_gather | solution.py:21
  218.3 48.3 %all-gather.5 = bf16[1,1024,128]{2,1,0:T(8,128)(2,1)S(1)} all-gather(bf16[1,16,128]{2,1,0:T(8,128)(2,1)S(1)} %get-tuple-element.17), channel_id=7, replica_groups=mesh['wide'=64,'narrow'=8] {'wide'}, dimensions={1}, use_global_device_ids=true | all-gather | bytes 266240 | tf_op jit(solution)/shard_map/all_gather | solution.py:25
  266.9 30.0 %all-gather.17.cloned.1.call-done = bf16[1024,512]{1,0:T(8,128)(2,1)} async-done(((bf16[16,512]{1,0:T(8,128)(2,1)}), bf16[1024,512]{1,0:T(8,128)(2,1)}) %all-gather.17.cloned.1.call-update) | async-done | bytes 1048592 | tf_op jit(solution)/shard_map/all_gather | solution.py:26
  296.9 1.7 convolution_convert_fusion.1
  298.8 13.1 %all-gather.6 = f32[128,512]{1,0:T(8,128)S(1)} all-gather(f32[16,512]{1,0:T(8,128)S(1)} %fusion.2), channel_id=8, replica_groups=mesh['wide'=64,'narrow'=8] {'narrow'}, dimensions={0}, use_global_device_ids=true | all-gather | bytes 294912 | tf_op jit(solution)/shard_map/all_gather | solution.py:21
  312.6 48.3 %all-gather.7 = bf16[1,1024,128]{2,1,0:T(8,128)(2,1)S(1)} all-gather(bf16[1,16,128]{2,1,0:T(8,128)(2,1)S(1)} %get-tuple-element.14), channel_id=9, replica_groups=mesh['wide'=64,'narrow'=8] {'wide'}, dimensions={1}, use_global_device_ids=true | all-gather | bytes 266240 | tf_op jit(solution)/shard_map/all_gather | solution.py:25
  360.9 30.3 %all-gather.19.cloned.1.call-done = bf16[1024,512]{1,0:T(8,128)(2,1)} async-done(((bf16[16,512]{1,0:T(8,128)(2,1)}), bf16[1024,512]{1,0:T(8,128)(2,1)}) %all-gather.19.cloned.1.call-update) | async-done | bytes 1048592 | tf_op jit(solution)/shard_map/all_gather | solution.py:26
  391.2 1.7 fusion.1
  392.9 3.2 convolution_bitcast_fusion
  396.2 1.0 copy.26
  397.3 39.8 %reduce-scatter.2.cloned.1.call-done = f32[256,512]{0,1:T(8,128)} async-done(((f32[2048,512]{0,1:T(8,128)}), f32[256,512]{0,1:T(8,128)}) %reduce-scatter.2.cloned.1.call-update) | async-done | bytes 524304 | tf_op jit(solution)/shard_map/reduce_scatter | solution.py:35
  437.1 2.0 copy.27
  (30 shorter events, 3.1 us)
Async XLA Ops:
  7.2 385.7 %copy-start = (bf16[2048,4,128]{2,1,0:T(4,128)(2,1)S(1)}, bf16[2048,4,128]{2,1,0:T(4,128)(2,1)}, u32[]{:S(2)}) copy-start(bf16[2048,4,128]{2,1,0:T(4,128)(2,1)} %param.9) | copy-start | bytes 6291460
  7.2 102.9 %copy-start.1 = (f32[1,4,16,512]{3,2,1,0:T(8,128)S(1)}, f32[1,4,16,512]{3,2,1,0:T(8,128)}, u32[]{:S(2)}) copy-start(f32[1,4,16,512]{3,2,1,0:T(8,128)} %param.6) | copy-start | bytes 393220
  7.2 116.2 %copy-start.2 = (bf16[4,16,512]{2,1,0:T(8,128)(2,1)S(1)}, bf16[4,16,512]{2,1,0:T(8,128)(2,1)}, u32[]{:S(2)}) copy-start(bf16[4,16,512]{2,1,0:T(8,128)(2,1)} %param.5) | copy-start | bytes 196612
  7.2 101.1 %all-gather.13.cloned.1.call-start = ((), (), s32[]{:S(2)}) async-start(), calls=%async_computation.1 | async-start | bytes 1064960 | tf_op jit(solution)/shard_map/all_gather | solution.py:26
  22.7 179.9 %all-gather.15.cloned.1.call-start = ((), (), s32[]{:S(2)}) async-start(), calls=%async_computation.2 | async-start | bytes 1064960 | tf_op jit(solution)/shard_map/all_gather | solution.py:26
  124.0 172.9 %all-gather.17.cloned.1.call-start = ((), (), s32[]{:S(2)}) async-start(), calls=%async_computation.3 | async-start | bytes 1064960 | tf_op jit(solution)/shard_map/all_gather | solution.py:26
  218.3 172.9 %all-gather.19.cloned.1.call-start = ((), (), s32[]{:S(2)}) async-start(), calls=%async_computation.4 | async-start | bytes 1064960 | tf_op jit(solution)/shard_map/all_gather | solution.py:26
  312.6 124.5 %reduce-scatter.2.cloned.1.call-start = ((), (), s32[]{:S(2)}) async-start(), calls=%async_computation.5 | async-start | bytes 4718592 | tf_op jit(solution)/shard_map/reduce_scatter | solution.py:35
Sparse Core Ops, SparseCore 0:
  22.8 85.4 all-gather.12
  124.1 78.4 all-gather.14
  218.4 78.4 all-gather.16
  312.7 78.4 all-gather.18
  396.3 40.7 reduce-scatter.1
